TPU v7x, 32 devices: a whole 2x2x4 slice. The times are simulated.
32 devices in a mesh: dp: 8 (over z, core), tensor: 4 (over y, x).
Axes of the slice: x: 2, y: 2, z: 4, core: 2. Of those that a mesh axis runs over, the one named last changes fastest.
Arguments:
- tokens: bfloat16 [8192, 2048], P('dp'), may hold values from -6 to 6
- lengths: int32 [64], P('dp'), may hold values from 1 to 64, 2560 in all
- cotangent: bfloat16 [8192, 2048], P('dp'), may hold values from -6 to 6
- pre_gain: float32 [2048], replicated, may hold values from 0.5 to 1.5
- pre_shift: float32 [2048], replicated, may hold values from -1.5 to 1.5
- qkv_weight: bfloat16 [3, 2048, 2048], P(None, None, 'tensor'), may hold values from -0.125 to 0.125
- qkv_bias: float32 [3, 2048], P(None, 'tensor'), may hold values from -1.5 to 1.5
- mix_gain: float32 [2048], P('tensor'), may hold values from 0.5 to 1.5
- mix_shift: float32 [2048], P('tensor'), may hold values from -1.5 to 1.5
- out_weight: bfloat16 [2048, 2048], P('tensor'), may hold values from -0.125 to 0.125
- out_bias: float32 [2048], replicated, may hold values from -1.5 to 1.5
- ffn_gain: float32 [2048], replicated, may hold values from 0.5 to 1.5
- ffn_shift: float32 [2048], replicated, may hold values from -1.5 to 1.5
- up_weight: bfloat16 [2048, 8192], P(None, 'tensor'), may hold values from -0.125 to 0.125
- up_bias: float32 [8192], P('tensor'), may hold values from -2.5 to 2.5
- hid_gain: float32 [8192], P('tensor'), may hold values from 0.5 to 1.5
- hid_shift: float32 [8192], P('tensor'), may hold values from -1.5 to 1.5
- down_weight: bfloat16 [8192, 2048], P('tensor'), may hold values from -0.0625 to 0.0625
- down_bias: float32 [2048], replicated, may hold values from -1.5 to 1.5
Outputs:
- output: bfloat16 [8192, 2048], P('dp')
- tokens_grad: float32 [8192, 2048], P('dp')
- pre_gain_grad: float32 [2048], replicated
- pre_shift_grad: float32 [2048], replicated
- qkv_weight_grad: float32 [3, 2048, 2048], P(None, 'dp', 'tensor')
- qkv_bias_grad: float32 [3, 2048], P(None, 'tensor')
- mix_gain_grad: float32 [2048], P('tensor')
- mix_shift_grad: float32 [2048], P('tensor')
- out_weight_grad: float32 [2048, 2048], P('tensor', 'dp')
- out_bias_grad: float32 [2048], replicated
- ffn_gain_grad: float32 [2048], replicated
- ffn_shift_grad: float32 [2048], replicated
- up_weight_grad: float32 [2048, 8192], P('dp', 'tensor')
- up_bias_grad: float32 [8192], P('tensor')
- hid_gain_grad: float32 [8192], P('tensor')
- hid_shift_grad: float32 [8192], P('tensor')
- down_weight_grad: float32 [8192, 2048], P('tensor', 'dp')
- down_bias_grad: float32 [2048], replicated
Inputs may be any that keep to these rules, and one draw needn't show every extreme that they name: Caption length of each pair; the lengths sum to 2560 and the longest is 64.
All inputs are finite; a program needn't handle non-finite values. No bound on the sum of `lengths` on one device may be relied on, other than what follows from the above.
Results may differ from a plain program's by a relative error of at most 0.013.
Values sent between devices are 32-bit elements; how exact they have to be, the bound alone decides.
No kernel may reach another device: no remote copies, remote signals or barrier semaphores. Data moves between devices by JAX's collectives and lax.ppermute only.
A program may use at most 256 MiB of HBM per device.

v0:
```python
import math
import jax
import jax.numpy as jnp
from jax import lax
from jax.sharding import PartitionSpec as P

D = 2048
HD = 64
FF = 8192
SLOT = 128
IMG = 64
SCALE_BASE = 512
eps = 1e-05
root_half = 0.7071067811865476
inv_root_two_pi = 0.3989422804014327
masked_score = -1e30


def rounded(value):
    return value.astype(jnp.bfloat16)


def tables():
    place = jnp.arange(SLOT, dtype=jnp.float32)
    index = jnp.arange(HD // 2, dtype=jnp.float32)
    theta = 10000.0 ** (-2.0 * index / HD)
    angle = place[:, None] * theta[None, :]
    zeta = (2.0 * index + 0.4 * HD) / (1.4 * HD)
    growth = zeta[None, :] ** ((place[:, None] - SLOT // 2) / SCALE_BASE)
    return (jnp.cos(angle), jnp.sin(angle), growth)


def rotate(value, cosine, sine, factor):
    shape = value.shape
    pairs = value.reshape(shape[:-1] + (shape[-1] // 2, 2))
    even = pairs[..., 0]
    odd = pairs[..., 1]
    cos_b = cosine[:, None, :]
    sin_b = sine[:, None, :]
    fac_b = factor[:, None, :]
    new_even = (even * cos_b - odd * sin_b) * fac_b
    new_odd = (odd * cos_b + even * sin_b) * fac_b
    return jnp.stack([new_even, new_odd], axis=-1).reshape(shape)


def local_norm(value):
    mean = jnp.mean(value, axis=-1, keepdims=True)
    var = jnp.mean(value * value, axis=-1, keepdims=True) - mean * mean
    inverse = lax.rsqrt(var + eps)
    return ((value - mean) * inverse, inverse)


def local_back(grad, hat, gain, inverse):
    scaled = grad * gain
    return inverse * (
        scaled
        - jnp.mean(scaled, axis=-1, keepdims=True)
        - hat * jnp.mean(scaled * hat, axis=-1, keepdims=True)
    )


def body(
    tokens,
    lengths,
    cotangent,
    pre_gain,
    pre_shift,
    qkv_weight,
    qkv_bias,
    mix_gain,
    mix_shift,
    out_weight,
    out_bias,
    ffn_gain,
    ffn_shift,
    up_weight,
    up_bias,
    hid_gain,
    hid_shift,
    down_weight,
    down_bias,
):
    pairs = lengths.shape[0]
    rows = tokens.shape[0]
    local_width = qkv_weight.shape[2]
    local_heads = local_width // HD
    scale = 1.0 / math.sqrt(HD)
    cosine, sine, growth = tables()
    shrink = 1.0 / growth
    place = jnp.arange(SLOT, dtype=jnp.int32)
    causal = (place[None, :] <= place[:, None])[None, None]
    valid = place[None, None, None, :] < (IMG + lengths)[:, None, None, None]
    allowed = causal & valid
    inputs = tokens.astype(jnp.float32)
    pre_hat, pre_inv = local_norm(inputs)
    first = rounded(pre_hat * pre_gain + pre_shift)
    proj = (
        jnp.einsum("td,cde->cte", first, qkv_weight, preferred_element_type=jnp.float32)
        + qkv_bias[:, None, :]
    )
    shaped = proj.reshape(3, pairs, SLOT, local_heads, HD)
    query = rounded(rotate(shaped[0], cosine, sine, growth))
    key = rounded(rotate(shaped[1], cosine, sine, shrink))
    value = rounded(shaped[2])

    def scores_of():
        raw = jnp.einsum("pqhd,pkhd->phqk", query, key, preferred_element_type=jnp.float32) * scale
        return jnp.where(allowed, raw, masked_score)

    scores = scores_of()
    top = jnp.max(scores, axis=-1, keepdims=True)
    expd = jnp.exp(scores - top)
    total = jnp.sum(expd, axis=-1, keepdims=True)
    probs = expd / total
    log_total = top + jnp.log(total)
    mixed = jnp.einsum(
        "phqk,pkhd->pqhd", rounded(probs), value, preferred_element_type=jnp.float32
    ).reshape(rows, local_width)
    mix_sums = lax.psum((jnp.sum(mixed, 1), jnp.sum(mixed * mixed, 1)), "tensor")
    mix_mean = mix_sums[0] / D
    mix_inv = lax.rsqrt(mix_sums[1] / D - mix_mean * mix_mean + eps)
    mix_hat = (mixed - mix_mean[:, None]) * mix_inv[:, None]
    mix_low = rounded(mix_hat * mix_gain + mix_shift)
    branch = lax.psum(jnp.dot(mix_low, out_weight, preferred_element_type=jnp.float32), "tensor")
    middle = inputs + branch + out_bias
    ffn_hat, ffn_inv = local_norm(middle)
    second = rounded(ffn_hat * ffn_gain + ffn_shift)
    hidden = jnp.dot(second, up_weight, preferred_element_type=jnp.float32) + up_bias
    active = jax.nn.gelu(hidden, approximate=False)
    hid_sums = lax.psum((jnp.sum(active, 1), jnp.sum(active * active, 1)), "tensor")
    hid_mean = hid_sums[0] / FF
    hid_inv = lax.rsqrt(hid_sums[1] / FF - hid_mean * hid_mean + eps)
    hid_hat = (active - hid_mean[:, None]) * hid_inv[:, None]
    hid_low = rounded(hid_hat * hid_gain + hid_shift)
    result = lax.psum(jnp.dot(hid_low, down_weight, preferred_element_type=jnp.float32), "tensor")
    final = middle + result + down_bias
    output = rounded(final)
    upstream = cotangent.astype(jnp.float32)
    down_grad = jnp.einsum("tf,td->fd", hid_low, cotangent, preferred_element_type=jnp.float32)
    down_bias_grad = jnp.sum(upstream, 0)
    hid_back = jnp.einsum("td,fd->tf", cotangent, down_weight, preferred_element_type=jnp.float32)
    hid_gain_grad = jnp.sum(hid_back * hid_hat, 0)
    hid_shift_grad = jnp.sum(hid_back, 0)
    hid_scaled = hid_back * hid_gain
    hid_back_sums = lax.psum((jnp.sum(hid_scaled, 1), jnp.sum(hid_scaled * hid_hat, 1)), "tensor")
    active_grad = hid_inv[:, None] * (
        hid_scaled - hid_back_sums[0][:, None] / FF - hid_hat * hid_back_sums[1][:, None] / FF
    )
    slope = 0.5 * (1.0 + lax.erf(hidden * root_half)) + hidden * inv_root_two_pi * jnp.exp(
        -0.5 * hidden * hidden
    )
    hidden_grad = rounded(active_grad * slope)
    up_grad = jnp.einsum("td,tf->df", second, hidden_grad, preferred_element_type=jnp.float32)
    up_bias_grad = jnp.sum(hidden_grad, 0, dtype=jnp.float32)
    second_grad = lax.psum(
        jnp.einsum("tf,df->td", hidden_grad, up_weight, preferred_element_type=jnp.float32),
        "tensor",
    )
    ffn_gain_grad = jnp.sum(second_grad * ffn_hat, 0)
    ffn_shift_grad = jnp.sum(second_grad, 0)
    middle_grad = upstream + local_back(second_grad, ffn_hat, ffn_gain, ffn_inv)
    branch_low = rounded(middle_grad)
    out_bias_grad = jnp.sum(middle_grad, 0)
    out_grad = jnp.einsum("te,td->ed", mix_low, branch_low, preferred_element_type=jnp.float32)
    mix_back = jnp.einsum("td,ed->te", branch_low, out_weight, preferred_element_type=jnp.float32)
    mix_gain_grad = jnp.sum(mix_back * mix_hat, 0)
    mix_shift_grad = jnp.sum(mix_back, 0)
    mix_scaled = mix_back * mix_gain
    mix_back_sums = lax.psum((jnp.sum(mix_scaled, 1), jnp.sum(mix_scaled * mix_hat, 1)), "tensor")
    mixed_grad = mix_inv[:, None] * (
        mix_scaled - mix_back_sums[0][:, None] / D - mix_hat * mix_back_sums[1][:, None] / D
    )
    mixed_grad = rounded(mixed_grad).reshape(pairs, SLOT, local_heads, HD)
    again = jnp.exp(scores_of() - log_total)
    prob_grad = jnp.einsum("pqhd,pkhd->phqk", mixed_grad, value, preferred_element_type=jnp.float32)
    carried = jnp.sum(again * prob_grad, axis=-1, keepdims=True)
    score_grad = rounded(again * (prob_grad - carried))
    query_grad = (
        jnp.einsum("phqk,pkhd->pqhd", score_grad, key, preferred_element_type=jnp.float32) * scale
    )
    key_grad = (
        jnp.einsum("phqk,pqhd->pkhd", score_grad, query, preferred_element_type=jnp.float32) * scale
    )
    value_grad = jnp.einsum(
        "phqk,pqhd->pkhd", rounded(again), mixed_grad, preferred_element_type=jnp.float32
    )
    query_pre = rotate(query_grad, cosine, -sine, growth)
    key_pre = rotate(key_grad, cosine, -sine, shrink)
    proj_grad = rounded(jnp.stack([query_pre, key_pre, value_grad]).reshape(3, rows, local_width))
    qkv_grad = jnp.einsum("td,cte->cde", first, proj_grad, preferred_element_type=jnp.float32)
    qkv_bias_grad = jnp.sum(proj_grad, 1, dtype=jnp.float32)
    first_grad = lax.psum(
        jnp.einsum("cte,cde->td", proj_grad, qkv_weight, preferred_element_type=jnp.float32),
        "tensor",
    )
    pre_gain_grad = jnp.sum(first_grad * pre_hat, 0)
    pre_shift_grad = jnp.sum(first_grad, 0)
    tokens_grad = middle_grad + local_back(first_grad, pre_hat, pre_gain, pre_inv)
    qkv_part, out_part, up_part, down_part = (
        lax.psum_scatter(qkv_grad, "dp", scatter_dimension=1, tiled=True),
        lax.psum_scatter(out_grad, "dp", scatter_dimension=1, tiled=True),
        lax.psum_scatter(up_grad, "dp", scatter_dimension=0, tiled=True),
        lax.psum_scatter(down_grad, "dp", scatter_dimension=1, tiled=True),
    )
    small = lax.psum(
        (
            pre_gain_grad,
            pre_shift_grad,
            qkv_bias_grad,
            mix_gain_grad,
            mix_shift_grad,
            out_bias_grad,
            ffn_gain_grad,
            ffn_shift_grad,
            up_bias_grad,
            hid_gain_grad,
            hid_shift_grad,
            down_bias_grad,
        ),
        "dp",
    )
    return (
        output,
        tokens_grad,
        small[0],
        small[1],
        qkv_part,
        small[2],
        small[3],
        small[4],
        out_part,
        small[5],
        small[6],
        small[7],
        up_part,
        small[8],
        small[9],
        small[10],
        down_part,
        small[11],
    )


def solution(mesh):
    in_specs = (
        P("dp", None),
        P("dp"),
        P("dp", None),
        P(),
        P(),
        P(None, None, "tensor"),
        P(None, "tensor"),
        P("tensor"),
        P("tensor"),
        P("tensor", None),
        P(),
        P(),
        P(),
        P(None, "tensor"),
        P("tensor"),
        P("tensor"),
        P("tensor"),
        P("tensor", None),
        P(),
    )
    out_specs = (
        P("dp", None),
        P("dp", None),
        P(),
        P(),
        P(None, "dp", "tensor"),
        P(None, "tensor"),
        P("tensor"),
        P("tensor"),
        P("tensor", "dp"),
        P(),
        P(),
        P(),
        P("dp", "tensor"),
        P("tensor"),
        P("tensor"),
        P("tensor"),
        P("tensor", "dp"),
        P(),
    )
    return jax.shard_map(body, mesh=mesh, in_specs=in_specs, out_specs=out_specs, check_vma=False)
```

profile of v0, /device:TPU:0, one launch (start us, length us, event | category | flops | bytes accessed | tf_op | source)
XLA Modules:
  0.0 1522.1 jit_solution(11128239787350795962)
XLA Ops:
  7.3 3.6 convert_reduce_fusion
  10.9 11.5 add_bitcast_fusion
  22.5 2.4 fusion.64
  26.0 2.9 copy.54
  28.9 3.4 copy.96
  32.3 2.9 copy.56
  44.1 3.9 reshape.336
  48.0 3.2 copy.58
  57.1 3.9 copy.84
  60.9 4.8 reshape.334
  65.7 11.5 all-reduce.4
  77.3 7.4 fusion.52
  84.9 171.4 %all-reduce.11.cloned.1.call-done = f32[1024,2048]{1,0:T(8,128)} async-done(((f32[1024,2048]{1,0:T(8,128)}), f32[1024,2048]{1,0:T(8,128)}) %all-reduce.11.cloned.1.call-update) | async-done | bytes 8388624 | tf_op jit(solution)/shard_map/psum | solution.py:124
  256.3 5.6 fusion.58
  262.0 36.0 %fusion.57 = (f32[1024]{0:T(1024)S(1)}, f32[1024]{0:T(1024)S(1)}, f32[1024,2048]{1,0:T(8,128)}, f32[1024,2048]{1,0:T(8,128)}) fusion(f32[2048]{0:T(1024)S(1)} %copy-done.37, bf16[2048,2048]{1,0:T(8,128)(2,1)} %param.32, f32[1024,2048]{1,0:T(8,128)S(1)} %get-tuple-element.105, f32[2048]{0:T(1024)S(1)} %copy-done.44, f32[2048]{0:T(1024)S(1)} %copy-done.30, ...), kind=kOutput, calls=%fused_computation.139 | convolution fusion | flops 8743024640 | bytes 33595392 | tf_op jit(solution)/shard_map/dot_general | solution.py:128
  298.0 9.8 all-reduce.3
  307.8 17.3 %multiply_reduce_fusion = (f32[2048]{0:T(1024)}, f32[1024]{0:T(1024)S(1)}, f32[1024]{0:T(1024)S(1)}, f32[2048]{0:T(1024)}, f32[1024,2048]{1,0:T(8,128)}) fusion(f32[1024,2048]{1,0:T(8,128)} %get-tuple-element.104, f32[1024]{0:T(1024)S(1)} %get-tuple-element.126, f32[1024]{0:T(1024)S(1)} %get-tuple-element.125, f32[2048]{0:T(1024)S(1)} %copy-done.38, ...), kind=kOutput, calls=%fused_computation.29 | convolution fusion | flops 8608802816 | bytes 29401088 | tf_op jit(solution)/shard_map/td,fd->tf/dot_general | solution.py:141
  325.1 8.1 all-reduce.2
  333.2 12.3 convert_reduce_fusion.2
  347.5 13.2 fusion.68
  361.4 15.9 %fusion.56 = f32[1024,2048]{1,0:T(8,128)} fusion(bf16[2048,2048]{1,0:T(8,128)(2,1)} %param.36, f32[1024,2048]{1,0:T(8,128)} %get-tuple-element.104, f32[2048]{0:T(1024)S(1)} %copy-done.43, f32[2048]{0:T(1024)S(1)} %copy-done.38, f32[1024]{0:T(1024)S(1)} %get-tuple-element.126, f32[1024]{0:T(1024)S(1)} %get-tuple-element.125), kind=kOutput, calls=%fused_computation.138 | convolution fusion | flops 8600420352 | bytes 25190400 | tf_op jit(solution)/shard_map/dot_general | solution.py:135
  377.4 155.8 %all-reduce.13.cloned.1.call-done = f32[1024,2048]{1,0:T(8,128)} async-done(((f32[1024,2048]{1,0:T(8,128)}), f32[1024,2048]{1,0:T(8,128)}) %all-reduce.13.cloned.1.call-update) | async-done | bytes 8388624 | tf_op jit(solution)/shard_map/psum | solution.py:155
  533.1 8.3 multiply_reduce_fusion.1
  542.6 7.6 fusion.61
  550.2 4.6 multiply_reduce_fusion.10
  554.8 9.8 all-reduce.1
  564.6 2.7 multiply_convert_fusion.1
  570.0 3.8 multiply_reduce_fusion.9
  577.5 2.5 fusion.43
  580.0 2.4 fusion.66
  582.4 2.4 fusion.65
  584.9 5.2 multiply_convert_fusion.5
  597.8 11.4 convolution_bitcast_fusion.1
  610.7 12.5 convolution_bitcast_fusion
  624.8 8.3 fusion.33
  633.3 2.6 convert_reduce_fusion.3
  635.9 280.1 %all-reduce.17.cloned.1.call-done = (f32[1024,2048]{1,0:T(8,128)}, f32[1024,2048]{1,0:T(8,128)}) async-done(((f32[1024,2048]{1,0:T(8,128)}, f32[1024,2048]{1,0:T(8,128)}), (f32[1024,2048]{1,0:T(8,128)}, f32[1024,2048]{1,0:T(8,128)})) %all-reduce.17.cloned.1.call-update) | async-done | bytes 16777232 | tf_op jit(solution)/shard_map/psum | solution.py:135
  916.0 7.1 fusion.18
  923.2 17.5 %fusion.55 = f32[2048,2048]{1,0:T(8,128)} fusion(bf16[1024,2048]{1,0:T(8,128)(2,1)} %param.21, f32[1024,2048]{1,0:T(8,128)} %get-tuple-element.104, f32[2048]{0:T(1024)S(1)} %copy-done.43, f32[2048]{0:T(1024)S(1)} %copy-done.38, f32[1024]{0:T(1024)S(1)} %get-tuple-element.126, f32[1024]{0:T(1024)S(1)} %get-tuple-element.125), kind=kOutput, calls=%fused_computation.137 | convolution fusion | flops 8600420352 | bytes 29384704 | tf_op jit(solution)/shard_map/tf,td->fd/dot_general | solution.py:139
  941.5 16.4 %fusion.53 = f32[2048,2048]{1,0:T(8,128)} fusion(bf16[1024,2048]{1,0:T(8,128)(2,1)} %copy-done.14, f32[1024,2048]{1,0:T(8,128)} %copy-done.2, f32[2048]{0:T(1024)S(1)} %copy-done.45, f32[2048]{0:T(1024)S(1)} %copy-done.30, f32[1024]{0:T(1024)S(1)} %get-tuple-element.128, f32[1024]{0:T(1024)S(1)} %get-tuple-element.127), kind=kOutput, calls=%fused_computation.135 | convolution fusion | flops 8600420352 | bytes 29384704 | tf_op jit(solution)/shard_map/td,tf->df/dot_general | solution.py:153
  958.6 10.4 add_convert_fusion
  969.0 9.7 fusion.17
  978.7 69.7 %reduce-scatter.5.cloned.1.call-done = f32[3,256,512]{1,2,0:T(8,128)} async-done(((f32[3,2048,512]{1,2,0:T(8,128)}), f32[3,256,512]{1,2,0:T(8,128)}) %reduce-scatter.5.cloned.1.call-update) | async-done | bytes 1572880 | tf_op jit(solution)/shard_map/reduce_scatter | solution.py:200
  1048.4 3.0 copy.78
  1051.4 48.1 %reduce-scatter.7.cloned.1.call-done = f32[512,256]{1,0:T(8,128)} async-done(((f32[512,2048]{1,0:T(8,128)}), f32[512,256]{1,0:T(8,128)}) %reduce-scatter.7.cloned.1.call-update) | async-done | bytes 524304 | tf_op jit(solution)/shard_map/reduce_scatter | solution.py:201
  1099.5 56.9 %all-reduce.15.cloned.1.call-done = (f32[2048]{0:T(1024)}, f32[2048]{0:T(1024)}, f32[3,512]{1,0:T(4,128)}, f32[512]{0:T(512)}, f32[512]{0:T(512)}, /*index=5*/f3...) async-done(((f32[2048]{0:T(1024)}, f32[2048]{0:T(1024)}, f32[3,512]{1,0:T(4,128)}, ...) | async-done | bytes 83984 | tf_op jit(solution)/shard_map/psum | solution.py:205
  1156.4 173.4 %reduce-scatter.11.cloned.1.call-done = f32[2048,256]{1,0:T(8,128)} async-done(((f32[2048,2048]{1,0:T(8,128)}), f32[2048,256]{1,0:T(8,128)}) %reduce-scatter.11.cloned.1.call-update) | async-done | bytes 2097168 | tf_op jit(solution)/shard_map/reduce_scatter | solution.py:203
  1329.8 169.6 %reduce-scatter.9.cloned.1.call-done = f32[256,2048]{1,0:T(8,128)} async-done(((f32[2048,2048]{1,0:T(8,128)}), f32[256,2048]{1,0:T(8,128)}) %reduce-scatter.9.cloned.1.call-update) | async-done | bytes 2097168 | tf_op jit(solution)/shard_map/reduce_scatter | solution.py:202
  (169 shorter events, 53.9 us)
Async XLA Ops:
  7.2 70.1 %copy-start = (bf16[512,2048]{1,0:T(8,128)(2,1)S(1)}, bf16[512,2048]{1,0:T(8,128)(2,1)}, u32[]{:S(2)}) copy-start(bf16[512,2048]{1,0:T(8,128)(2,1)} %param.28) | copy-start | bytes 6291460
  7.2 249.1 %all-reduce.11.cloned.1.call-start = ((), (), s32[]{:S(2)}) async-start(), calls=%async_computation.4 | async-start | bytes 16777216 | tf_op jit(solution)/shard_map/psum | solution.py:124
  10.9 11.6 copy-start.26
  10.9 11.6 copy-start.28
  37.2 6.8 copy-start.48
  38.0 6.0 copy-start.19
  38.1 5.9 copy-start.21
  38.1 5.9 copy-start.23
  41.7 12.0 copy-start.8
  51.2 3.6 copy-start.15
  53.7 3.4 copy-start.3
  57.1 20.2 %copy-start.40 = (f32[512]{0:T(512)S(1)}, f32[512]{0:T(512)}, u32[]{:S(2)}) copy-start(f32[512]{0:T(512)} %param.26) | copy-start | bytes 6148
  57.1 20.2 %copy-start.46 = (f32[512]{0:T(512)S(1)}, f32[512]{0:T(512)}, u32[]{:S(2)}) copy-start(f32[512]{0:T(512)} %param.27) | copy-start | bytes 6148
  77.3 7.5 copy-start.32
  77.3 7.5 copy-start.34
  77.3 179.0 %copy-start.36 = (f32[2048]{0:T(1024)S(1)}, f32[2048]{0:T(1024)}, u32[]{:S(2)}) copy-start(f32[2048]{0:T(1024)} %param.29) | copy-start | bytes 24580
  84.8 177.2 %copy-start.30 = (f32[2048]{0:T(1024)S(1)}, f32[2048]{0:T(1024)}, u32[]{:S(2)}) copy-start(f32[2048]{0:T(1024)} %param.30) | copy-start | bytes 24580
  84.8 177.2 %copy-start.37 = (f32[2048]{0:T(1024)S(1)}, f32[2048]{0:T(1024)}, u32[]{:S(2)}) copy-start(f32[2048]{0:T(1024)} %param.33) | copy-start | bytes 24580
  84.8 177.2 %copy-start.44 = (f32[2048]{0:T(1024)S(1)}, f32[2048]{0:T(1024)}, u32[]{:S(2)}) copy-start(f32[2048]{0:T(1024)} %param.31) | copy-start | bytes 24580
  84.8 448.3 %all-reduce.13.cloned.1.call-start = ((), (), s32[]{:S(2)}) async-start(), calls=%async_computation.5 | async-start | bytes 16777216 | tf_op jit(solution)/shard_map/psum | solution.py:155
  261.9 36.0 %copy-start.2 = (f32[1024,2048]{1,0:T(8,128)}, f32[1024,2048]{1,0:T(8,128)S(1)}, u32[]{:S(2)}) copy-start(f32[1024,2048]{1,0:T(8,128)S(1)} %get-tuple-element.105) | copy-start | bytes 25165828
  262.0 45.8 %copy-start.38 = (f32[2048]{0:T(1024)S(1)}, f32[2048]{0:T(1024)}, u32[]{:S(2)}) copy-start(f32[2048]{0:T(1024)} %param.34) | copy-start | bytes 24580
  345.5 2.0 copy-start.14
  360.8 555.3 %all-reduce.17.cloned.1.call-start = ((), (), s32[]{:S(2)}) async-start(), calls=%async_computation.11 | async-start | bytes 33554432 | tf_op jit(solution)/shard_map/psum | solution.py:135
  533.1 8.4 copy-start.6
  533.1 9.4 copy-start.13
  542.5 7.6 copy-start.11
  542.5 7.6 copy-start.33
  542.5 7.6 copy-start.35
  542.5 7.6 copy-start.41
  550.2 4.7 copy-start.7
  570.0 3.9 copy-start.4
  570.0 5.2 copy-start.10
  573.9 2.9 copy-start.9
  577.4 7.4 copy-start.20
  577.4 7.4 copy-start.22
  577.5 7.4 copy-start.24
  577.5 7.4 copy-start.25
  584.8 10.5 copy-start.18
  609.2 439.2 %reduce-scatter.5.cloned.1.call-start = ((), (), s32[]{:S(2)}) async-start(), calls=%async_computation.6 | async-start | bytes 14155776 | tf_op jit(solution)/shard_map/reduce_scatter | solution.py:200
  623.2 1.6 copy-start.12
  623.2 1.6 copy-start.47
  623.2 476.3 %reduce-scatter.7.cloned.1.call-start = ((), (), s32[]{:S(2)}) async-start(), calls=%async_computation.7 | async-start | bytes 4718592 | tf_op jit(solution)/shard_map/reduce_scatter | solution.py:201
  633.1 523.3 %all-reduce.15.cloned.1.call-start = ((), (), s32[]{:S(2)}) async-start(), calls=%async_computation.10 | async-start | bytes 172032 | tf_op jit(solution)/shard_map/psum | solution.py:205
  923.2 406.6 %reduce-scatter.11.cloned.1.call-start = ((), (), s32[]{:S(2)}) async-start(), calls=%async_computation.9 | async-start | bytes 18874368 | tf_op jit(solution)/shard_map/reduce_scatter | solution.py:203
  940.8 558.6 %reduce-scatter.9.cloned.1.call-start = ((), (), s32[]{:S(2)}) async-start(), calls=%async_computation.8 | async-start | bytes 18874368 | tf_op jit(solution)/shard_map/reduce_scatter | solution.py:202
  958.6 10.4 copy-start.5
  969.0 545.8 %copy-start.1 = (bf16[512,2048]{1,0:T(8,128)(2,1)S(1)}, bf16[512,2048]{1,0:T(8,128)(2,1)}, u32[]{:S(2)}) copy-start(bf16[512,2048]{1,0:T(8,128)(2,1)} %param.28) | copy-start | bytes 6291460
  (9 other events, 11.0 us)
Sparse Core Ops, SparseCore 0:
  84.9 171.3 all-reduce.10
  360.9 172.1 all-reduce.12
  609.4 306.6 all-reduce.16
  918.2 130.1 reduce-scatter.4
  1051.1 48.3 reduce-scatter.6
  1104.5 51.8 all-reduce.14
  1159.3 170.4 reduce-scatter.10
  1332.8 166.6 reduce-scatter.8
where the time goes:
time: 1530 us; the launch traced here: 1520 us
  waiting for transfers between devices  1130 us (74%)
  matrix products  185 us (12%)
  other arithmetic  82.8 us (5%)
  local copies, waits for them, and re-layouts  73.6 us (5%)
  blocking collectives  39.2 us (3%)
  between operations  15.4 us (1%)
    psum x1, waiting for transfers between devices, body(): lax.psum(jnp.dot(hid_low, down_weight, preferred_element_type=jnp.float32...  280 us
    reduce_scatter x1, waiting for transfers between devices, body(): lax.psum_scatter(down_grad, 'dp', scatter_dimension=1, tiled=True)  173 us
    psum x1, waiting for transfers between devices, body(): lax.psum(jnp.dot(mix_low, out_weight, preferred_element_type=jnp.float32)...  171 us
    reduce_scatter x1, waiting for transfers between devices, body(): lax.psum_scatter(up_grad, 'dp', scatter_dimension=0, tiled=True)  170 us
    psum x1, waiting for transfers between devices, body(): lax.psum(jnp.einsum('tf,df->td', hidden_grad, up_weight, preferred_elemen...  156 us
    reduce_scatter x1, waiting for transfers between devices, body(): lax.psum_scatter(qkv_grad, 'dp', scatter_dimension=1, tiled=True)  69.7 us
    psum x1, waiting for transfers between devices, body(): lax.psum((pre_gain_grad, pre_shift_grad, qkv_bias_grad, mix_gain_grad, mi...  56.9 us
    reduce_scatter x1, waiting for transfers between devices, body(): lax.psum_scatter(out_grad, 'dp', scatter_dimension=1, tiled=True)  48.1 us
  transfers between devices with their start and end apart: 8, of which 8 were waited for; matrix products, arithmetic and copies ran while one was open for 7% of the time, Pallas kernels for 0%

commit v1 on v0

--- a/solution.py
+++ b/solution.py
@@ -132,7 +132,10 @@
     hid_inv = lax.rsqrt(hid_sums[1] / FF - hid_mean * hid_mean + eps)
     hid_hat = (active - hid_mean[:, None]) * hid_inv[:, None]
     hid_low = rounded(hid_hat * hid_gain + hid_shift)
-    result = lax.psum(jnp.dot(hid_low, down_weight, preferred_element_type=jnp.float32), "tensor")
+    result = jnp.sum(
+        lax.all_gather(jnp.dot(hid_low, down_weight, preferred_element_type=jnp.float32), "tensor"),
+        axis=0,
+    )
     final = middle + result + down_bias
     output = rounded(final)
     upstream = cotangent.astype(jnp.float32)

time: 1530 us -> 1720 us (1.12)
  waiting for transfers between devices: 1130 us -> 1290 us
  other arithmetic: 82.8 us -> 101 us
    all_gather x0 -> x1, waiting for transfers between devices: none -> 291 us  [body(): lax.all_gather(jnp.dot(hid_low, down_weight, preferred_element_type=jnp.f...]
    psum x1, waiting for transfers between devices: 280 us -> 112 us  [body(): lax.psum(jnp.einsum('cte,cde->td', proj_grad, qkv_weight, preferred_eleme...]
    reduce_scatter x1, waiting for transfers between devices: 69.7 us -> 112 us  [body(): lax.psum_scatter(qkv_grad, 'dp', scatter_dimension=1, tiled=True)]
  transfers between devices with their start and end apart: 8 -> 9, of which waited for: 8 -> 9; matrix products, arithmetic and copies ran while one was open for 7% -> 6% of each run, Pallas kernels for 0% -> 0%
where the time goes in v1:
time: 1720 us; the launch traced here: 1710 us
  waiting for transfers between devices  1290 us (75%)
  matrix products  185 us (11%)
  other arithmetic  101 us (6%)
  local copies, waits for them, and re-layouts  82.2 us (5%)
  blocking collectives  38.4 us (2%)
    all_gather x1, waiting for transfers between devices, body(): lax.all_gather(jnp.dot(hid_low, down_weight, preferred_element_type=jnp.f...  291 us
    psum x1, waiting for transfers between devices, body(): lax.psum(jnp.dot(mix_low, out_weight, preferred_element_type=jnp.float32)...  171 us
    reduce_scatter x1, waiting for transfers between devices, body(): lax.psum_scatter(up_grad, 'dp', scatter_dimension=0, tiled=True)  170 us
    reduce_scatter x1, waiting for transfers between devices, body(): lax.psum_scatter(down_grad, 'dp', scatter_dimension=1, tiled=True)  166 us
    psum x1, waiting for transfers between devices, body(): lax.psum(jnp.einsum('tf,df->td', hidden_grad, up_weight, preferred_elemen...  155 us
    psum x1, waiting for transfers between devices, body(): lax.psum(jnp.einsum('cte,cde->td', proj_grad, qkv_weight, preferred_eleme...  112 us
    reduce_scatter x1, waiting for transfers between devices, body(): lax.psum_scatter(qkv_grad, 'dp', scatter_dimension=1, tiled=True)  112 us
    psum x1, waiting for transfers between devices, body(): lax.psum((pre_gain_grad, pre_shift_grad, qkv_bias_grad, mix_gain_grad, mi...  57 us
  transfers between devices with their start and end apart: 9, of which 9 were waited for; matrix products, arithmetic and copies ran while one was open for 6% of the time, Pallas kernels for 0%

profile of v1, /device:TPU:0, one launch (start us, length us, event | category | flops | bytes accessed | tf_op | source)
XLA Modules:
  0.0 1708.8 jit_solution(16560110769707821327)
XLA Ops:
  7.3 3.6 convert_reduce_fusion
  10.9 11.5 add_bitcast_fusion
  26.0 2.9 copy.54
  28.9 3.4 copy.96
  32.3 2.9 copy.56
  44.1 3.9 reshape.337
  48.0 3.2 copy.58
  57.1 3.9 copy.84
  61.0 4.8 reshape.335
  65.8 11.5 all-reduce.4
  77.9 7.4 fusion.52
  85.4 171.5 %all-reduce.10.cloned.1.call-done = f32[1024,2048]{1,0:T(8,128)} async-done(((f32[1024,2048]{1,0:T(8,128)}), f32[1024,2048]{1,0:T(8,128)}) %all-reduce.10.cloned.1.call-update) | async-done | bytes 8388624 | tf_op jit(solution)/shard_map/psum | solution.py:124
  256.9 5.6 fusion.58
  262.6 36.0 %fusion.57 = (f32[1024]{0:T(1024)S(1)}, f32[1024]{0:T(1024)S(1)}, f32[1024,2048]{1,0:T(8,128)}, f32[1024,2048]{1,0:T(8,128)}) fusion(f32[2048]{0:T(1024)S(1)} %copy-done.34, bf16[2048,2048]{1,0:T(8,128)(2,1)} %param.32, f32[1024,2048]{1,0:T(8,128)S(1)} %get-tuple-element.103, f32[2048]{0:T(1024)S(1)} %copy-done.41, f32[2048]{0:T(1024)S(1)} %copy-done.27, ...), kind=kOutput, calls=%fused_computation.139 | convolution fusion | flops 8743024640 | bytes 33595392 | tf_op jit(solution)/shard_map/dot_general | solution.py:128
  298.6 9.8 all-reduce.3
  308.4 17.3 %multiply_reduce_fusion = (f32[2048]{0:T(1024)}, f32[1024]{0:T(1024)S(1)}, f32[1024]{0:T(1024)S(1)}, f32[2048]{0:T(1024)}, f32[1024,2048]{1,0:T(8,128)}) fusion(f32[1024,2048]{1,0:T(8,128)} %get-tuple-element.102, f32[1024]{0:T(1024)S(1)} %get-tuple-element.125, f32[1024]{0:T(1024)S(1)} %get-tuple-element.124, f32[2048]{0:T(1024)S(1)} %copy-done.35, ...), kind=kOutput, calls=%fused_computation.29 | convolution fusion | flops 8608802816 | bytes 29401088 | tf_op jit(solution)/shard_map/td,fd->tf/dot_general | solution.py:144
  325.7 8.1 all-reduce.2
  333.8 12.2 convert_reduce_fusion.2
  348.0 13.2 fusion.68
  361.9 16.0 fusion.56
  378.7 154.9 %all-reduce.12.cloned.1.call-done = f32[1024,2048]{1,0:T(8,128)} async-done(((f32[1024,2048]{1,0:T(8,128)}), f32[1024,2048]{1,0:T(8,128)}) %all-reduce.12.cloned.1.call-update) | async-done | bytes 8388624 | tf_op jit(solution)/shard_map/psum | solution.py:158
  533.6 8.2 multiply_reduce_fusion.1
  541.8 291.4 %all-gather.3.cloned.1.call-done = f32[4096,2048]{1,0:T(8,128)} async-done(((f32[1024,2048]{1,0:T(8,128)}), f32[4096,2048]{1,0:T(8,128)}) %all-gather.3.cloned.1.call-update) | async-done | bytes 33554448 | tf_op jit(solution)/shard_map/all_gather | solution.py:136
  833.3 15.9 reduce_sum.294
  849.2 15.0 fusion.61
  864.3 4.6 multiply_reduce_fusion.10
  868.9 9.1 all-reduce.1
  878.0 2.7 multiply_convert_fusion.1
  882.7 2.7 copy.63
  885.4 3.8 multiply_reduce_fusion.9
  892.9 2.5 fusion.43
  900.3 5.3 multiply_convert_fusion.5
  920.2 3.2 reshape.336
  923.4 11.4 convolution_bitcast_fusion.1
  935.5 12.8 convolution_bitcast_fusion
  948.4 16.6 fusion.55
  965.7 16.7 fusion.53
  983.1 8.6 fusion.33
  992.0 2.6 convert_reduce_fusion.3
  994.6 112.4 %all-reduce.14.cloned.1.call-done = f32[1024,2048]{1,0:T(8,128)} async-done(((f32[1024,2048]{1,0:T(8,128)}), f32[1024,2048]{1,0:T(8,128)}) %all-reduce.14.cloned.1.call-update) | async-done | bytes 8388624 | tf_op jit(solution)/shard_map/psum | solution.py:195
  1107.0 7.1 fusion.18
  1114.2 13.0 fusion.17
  1127.2 111.8 %reduce-scatter.5.cloned.1.call-done = f32[3,256,512]{1,2,0:T(8,128)} async-done(((f32[3,2048,512]{1,2,0:T(8,128)}), f32[3,256,512]{1,2,0:T(8,128)}) %reduce-scatter.5.cloned.1.call-update) | async-done | bytes 1572880 | tf_op jit(solution)/shard_map/reduce_scatter | solution.py:203
  1239.0 3.0 copy.78
  1242.1 166.4 %reduce-scatter.11.cloned.1.call-done = f32[2048,256]{1,0:T(8,128)} async-done(((f32[2048,2048]{1,0:T(8,128)}), f32[2048,256]{1,0:T(8,128)}) %reduce-scatter.11.cloned.1.call-update) | async-done | bytes 2097168 | tf_op jit(solution)/shard_map/reduce_scatter | solution.py:206
  1408.5 169.6 %reduce-scatter.9.cloned.1.call-done = f32[256,2048]{1,0:T(8,128)} async-done(((f32[2048,2048]{1,0:T(8,128)}), f32[256,2048]{1,0:T(8,128)}) %reduce-scatter.9.cloned.1.call-update) | async-done | bytes 2097168 | tf_op jit(solution)/shard_map/reduce_scatter | solution.py:205
  1578.0 51.3 %reduce-scatter.7.cloned.1.call-done = f32[512,256]{1,0:T(8,128)} async-done(((f32[512,2048]{1,0:T(8,128)}), f32[512,256]{1,0:T(8,128)}) %reduce-scatter.7.cloned.1.call-update) | async-done | bytes 524304 | tf_op jit(solution)/shard_map/reduce_scatter | solution.py:204
  1629.3 57.0 %all-reduce.16.cloned.1.call-done = (f32[2048]{0:T(1024)}, f32[2048]{0:T(1024)}, f32[3,512]{1,0:T(4,128)}, f32[512]{0:T(512)}, f32[512]{0:T(512)}, /*index=5*/f3...) async-done(((f32[2048]{0:T(1024)}, f32[2048]{0:T(1024)}, f32[3,512]{1,0:T(4,128)}, ...) | async-done | bytes 83984 | tf_op jit(solution)/shard_map/psum | solution.py:208
  (166 shorter events, 65.5 us)
Async XLA Ops:
  7.2 70.7 %copy-start = (bf16[512,2048]{1,0:T(8,128)(2,1)S(1)}, bf16[512,2048]{1,0:T(8,128)(2,1)}, u32[]{:S(2)}) copy-start(bf16[512,2048]{1,0:T(8,128)(2,1)} %param.28) | copy-start | bytes 6291460
  7.2 249.7 %all-reduce.10.cloned.1.call-start = ((), (), s32[]{:S(2)}) async-start(), calls=%async_computation.4 | async-start | bytes 16777216 | tf_op jit(solution)/shard_map/psum | solution.py:124
  10.9 11.6 copy-start.23
  10.9 11.6 copy-start.25
  37.2 6.8 copy-start.45
  38.0 6.0 copy-start.14
  38.1 5.9 copy-start.16
  38.1 5.9 copy-start.18
  41.7 12.0 copy-start.5
  51.2 3.6 copy-start.10
  53.7 3.3 copy-start.1
  53.7 3.3 copy-start.12
  54.8 2.3 copy-start.20
  57.1 20.8 %copy-start.37 = (f32[512]{0:T(512)S(1)}, f32[512]{0:T(512)}, u32[]{:S(2)}) copy-start(f32[512]{0:T(512)} %param.26) | copy-start | bytes 6148
  57.1 20.8 %copy-start.43 = (f32[512]{0:T(512)S(1)}, f32[512]{0:T(512)}, u32[]{:S(2)}) copy-start(f32[512]{0:T(512)} %param.27) | copy-start | bytes 6148
  77.9 179.0 %copy-start.33 = (f32[2048]{0:T(1024)S(1)}, f32[2048]{0:T(1024)}, u32[]{:S(2)}) copy-start(f32[2048]{0:T(1024)} %param.29) | copy-start | bytes 24580
  85.3 177.2 %copy-start.27 = (f32[2048]{0:T(1024)S(1)}, f32[2048]{0:T(1024)}, u32[]{:S(2)}) copy-start(f32[2048]{0:T(1024)} %param.30) | copy-start | bytes 24580
  85.4 177.2 %copy-start.34 = (f32[2048]{0:T(1024)S(1)}, f32[2048]{0:T(1024)}, u32[]{:S(2)}) copy-start(f32[2048]{0:T(1024)} %param.33) | copy-start | bytes 24580
  85.4 177.2 %copy-start.41 = (f32[2048]{0:T(1024)S(1)}, f32[2048]{0:T(1024)}, u32[]{:S(2)}) copy-start(f32[2048]{0:T(1024)} %param.31) | copy-start | bytes 24580
  85.4 448.2 %all-reduce.12.cloned.1.call-start = ((), (), s32[]{:S(2)}) async-start(), calls=%async_computation.5 | async-start | bytes 16777216 | tf_op jit(solution)/shard_map/psum | solution.py:158
  262.5 36.1 %copy-start.3 = (f32[1024,2048]{1,0:T(8,128)}, f32[1024,2048]{1,0:T(8,128)S(1)}, u32[]{:S(2)}) copy-start(f32[1024,2048]{1,0:T(8,128)S(1)} %get-tuple-element.103) | copy-start | bytes 25165828
  262.6 45.8 %copy-start.35 = (f32[2048]{0:T(1024)S(1)}, f32[2048]{0:T(1024)}, u32[]{:S(2)}) copy-start(f32[2048]{0:T(1024)} %param.34) | copy-start | bytes 24580
  346.0 2.0 copy-start.9
  361.2 472.0 %all-gather.3.cloned.1.call-start = ((), (), s32[]{:S(2)}) async-start(), calls=%async_computation.11 | async-start | bytes 41943040 | tf_op jit(solution)/shard_map/all_gather | solution.py:136
  377.9 0.8 copy-start.13
  377.9 0.8 copy-start.21
  378.0 729.1 %all-reduce.14.cloned.1.call-start = ((), (), s32[]{:S(2)}) async-start(), calls=%async_computation.6 | async-start | bytes 16777216 | tf_op jit(solution)/shard_map/psum | solution.py:195
  833.3 15.9 copy-start.36
  849.2 15.0 copy-start.8
  849.2 15.0 copy-start.30
  849.2 15.0 copy-start.32
  849.2 15.0 copy-start.38
  864.2 4.7 copy-start.4
  885.4 3.9 copy-start.2
  885.4 5.2 copy-start.7
  889.3 2.9 copy-start.6
  892.9 7.4 copy-start.15
  892.9 7.4 copy-start.17
  892.9 7.4 copy-start.19
  892.9 7.4 copy-start.22
  900.3 17.9 %copy-start.11 = (bf16[8,128,8,64]{1,3,2,0:T(8,128)(2,1)S(1)}, bf16[8,128,8,64]{1,3,2,0:T(8,128)(2,1)}, u32[]{:S(2)}) copy-start(bf16[8,128,8,64]{1,3,2,0:T(8,128)(2,1)} %fusion.43) | copy-start | bytes 3145732
  934.8 0.7 copy-start.28
  934.8 0.7 copy-start.39
  934.9 304.2 %reduce-scatter.5.cloned.1.call-start = ((), (), s32[]{:S(2)}) async-start(), calls=%async_computation.7 | async-start | bytes 14155776 | tf_op jit(solution)/shard_map/reduce_scatter | solution.py:203
  948.3 460.1 %reduce-scatter.11.cloned.1.call-start = ((), (), s32[]{:S(2)}) async-start(), calls=%async_computation.10 | async-start | bytes 18874368 | tf_op jit(solution)/shard_map/reduce_scatter | solution.py:206
  965.0 613.0 %reduce-scatter.9.cloned.1.call-start = ((), (), s32[]{:S(2)}) async-start(), calls=%async_computation.9 | async-start | bytes 18874368 | tf_op jit(solution)/shard_map/reduce_scatter | solution.py:205
  982.4 646.9 %reduce-scatter.7.cloned.1.call-start = ((), (), s32[]{:S(2)}) async-start(), calls=%async_computation.8 | async-start | bytes 4718592 | tf_op jit(solution)/shard_map/reduce_scatter | solution.py:204
  991.7 694.6 %all-reduce.16.cloned.1.call-start = ((), (), s32[]{:S(2)}) async-start(), calls=%async_computation.12 | async-start | bytes 172032 | tf_op jit(solution)/shard_map/psum | solution.py:208
  (7 other events, 4.6 us)
Sparse Core Ops, SparseCore 0:
  85.5 171.3 all-reduce.9
  361.4 172.2 all-reduce.11
  535.5 297.7 all-gather.2
  935.0 172.0 all-reduce.13
  1109.2 129.8 reduce-scatter.4
  1241.8 166.6 reduce-scatter.10
  1411.4 166.5 reduce-scatter.8
  1580.9 48.3 reduce-scatter.6
  1634.5 51.8 all-reduce.15
